TPU v7x, 32 devices: a whole 2x2x4 slice. The times are simulated.
32 devices in a mesh: row: 4 (over z), replica: 4 (over y, core), feat: 2 (over x).
Axes of the slice: x: 2, y: 2, z: 4, core: 2. Of those that a mesh axis runs over, the one named last changes fastest.
Arguments:
- features: bfloat16 [4, 4096, 256], P('replica', ('row', 'feat')), may hold values from -6 to 6
- tiles: bfloat16 [4, 32, 4, 3, 128, 128], P('replica', ('row', 'feat')), may hold values from 0 to 1
- block_cols: int32 [4, 32, 4, 3], P('replica', ('row', 'feat')), may hold values from 0 to 7
- block_counts: int32 [4, 32, 4], P('replica', ('row', 'feat')), may hold values from 0 to 3, as said below
- degrees: int32 [4, 4096], P('replica', ('row', 'feat')), may hold values from 32 to 287
- w_self: bfloat16 [256, 256], P(None, 'feat'), may hold values from -0.375 to 0.375
- w_neigh: bfloat16 [256, 256], P(None, 'feat'), may hold values from -0.375 to 0.375
- gamma: float32 [256], P('feat'), may hold values from 0.5 to 1.5
- beta: float32 [256], P('feat'), may hold values from -3 to 3
Outputs:
- hidden_out: bfloat16 [4, 4096, 256], P('replica', 'row', 'feat')
Inputs may be any that keep to these rules, and one draw needn't show every extreme that they name: `block_counts`: some block row uses all 3 slots of some source shard in every partition.
All inputs are finite; a program needn't handle non-finite values.
Results may differ from a plain program's by a relative error of at most 0.001.
Values may be sent and summed in bfloat16 or wider, within the bound.
No kernel may reach another device: no remote copies, remote signals or barrier semaphores. Data moves between devices by JAX's collectives and lax.ppermute only.
A program may use at most 128 MiB of HBM per device.

v0:
```python
import jax
import jax.numpy as jnp
from jax import lax
from jax.sharding import PartitionSpec as P


def per_device(features, tiles, block_cols, block_counts, degrees, w_self, w_neigh, gamma, beta):
    local_x = features[0]
    local_tiles = tiles[0]
    local_cols = block_cols[0]
    local_counts = block_counts[0]
    nodes_here = local_x.shape[0]
    width = local_x.shape[1]
    block_size = local_tiles.shape[3]
    slots = local_tiles.shape[2]
    row_blocks = local_tiles.shape[0]
    pair = lax.all_gather(local_x, "feat", axis=0, tiled=True)
    shard_rows = pair.shape[0]
    shard_blocks = shard_rows // block_size
    slot_index = jnp.arange(slots, dtype=jnp.int32)[None, :]
    start_total = jnp.zeros((row_blocks, block_size, width), jnp.float32)
    piece = lax.all_gather(pair, "row", axis=0, tiled=True)
    count_shards = piece.shape[0] // shard_rows
    shards = piece.reshape(count_shards, shard_blocks, block_size, width)

    def one_shard(step, acc):
        shard = lax.dynamic_index_in_dim(shards, step, 0, keepdims=False)
        counts_now = lax.dynamic_index_in_dim(local_counts, step, 1, keepdims=False)
        cols_now = lax.dynamic_index_in_dim(local_cols, step, 1, keepdims=False)
        tiles_now = lax.dynamic_index_in_dim(local_tiles, step, 1, keepdims=False)
        picked = shard[cols_now]
        used = slot_index < counts_now[:, None]
        masked = jnp.where(used[:, :, None, None], tiles_now, jnp.zeros((), tiles_now.dtype))
        return acc + jnp.einsum(
            "bcij,bcjf->bif", masked, picked, preferred_element_type=jnp.float32
        )

    agg_sum = lax.fori_loop(0, count_shards, one_shard, start_total).reshape(nodes_here, width)
    agg = (agg_sum / degrees[0][:, None].astype(jnp.float32)).astype(jnp.bfloat16)
    agg_pair = lax.all_gather(agg, "feat", axis=0, tiled=True)
    pre = jnp.dot(pair, w_self, preferred_element_type=jnp.float32) + jnp.dot(
        agg_pair, w_neigh, preferred_element_type=jnp.float32
    )
    col_sum, col_sq = lax.psum(
        (jnp.sum(pre, axis=0), jnp.sum(pre * pre, axis=0)), ("row", "replica")
    )
    total_nodes = pre.shape[0] * lax.axis_size("row") * lax.axis_size("replica")
    mean = col_sum / total_nodes
    var = col_sq / total_nodes - mean * mean
    normed = gamma * (pre - mean) / jnp.sqrt(var + 1e-05) + beta
    return jnp.maximum(normed, 0.0).astype(jnp.bfloat16)[None]


def solution(mesh):
    in_specs = (
        P("replica", ("row", "feat"), None),
        P("replica", ("row", "feat"), None, None, None, None),
        P("replica", ("row", "feat"), None, None),
        P("replica", ("row", "feat"), None),
        P("replica", ("row", "feat")),
        P(None, "feat"),
        P(None, "feat"),
        P("feat"),
        P("feat"),
    )
    out_specs = P("replica", "row", "feat")
    return jax.shard_map(
        per_device, mesh=mesh, in_specs=in_specs, out_specs=out_specs, check_vma=False
    )
```

profile of v0, /device:TPU:0, one launch (start us, length us, event | category | flops | bytes accessed | tf_op | source)
XLA Modules:
  0.0 121.8 jit_solution(17375432722191585981)
XLA Ops:
  6.5 0.0 copy-start
  6.5 0.0 all-gather.4.cloned.1.call-start
  6.5 12.0 %all-gather = bf16[1,1024,256]{2,1,0:T(8,128)(2,1)} all-gather(bf16[1,512,256]{2,1,0:T(8,128)(2,1)} %param.11), channel_id=2, replica_groups=mesh['row'=4,'replica'=4,'feat'=2] {'feat'}, dimensions={1}, use_global_device_ids=true | all-gather | bytes 786432 | tf_op jit(solution)/shard_map/all_gather | solution.py:17
  18.6 0.0 all-gather.4.cloned.1.call-update
  18.6 0.0 copy-start.4
  18.6 0.0 copy-start.5
  18.6 0.0 copy-start.6
  18.6 0.0 copy-start.1
  18.7 0.0 copy-start.3
  18.7 1.6 %copy.20 = bf16[1,4,4,3,128,128]{5,4,3,1,2,0:T(8,128)(2,1)S(1)} copy(bf16[1,4,4,3,128,128]{5,4,3,2,1,0:T(8,128)(2,1)} %param.12) | data formatting | bytes 3145728 | tf_op args[1]
  20.2 0.0 copy-done.4
  20.3 0.1 copy.17
  20.4 0.0 copy-done.5
  20.4 0.1 copy.16
  20.5 0.0 copy-done.6
  20.5 0.0 copy-done.1
  20.5 0.0 copy-done.3
  20.5 1.1 fusion.10
  21.6 43.2 %all-gather.4.cloned.1.call-done = bf16[1,4096,256]{2,1,0:T(8,128)(2,1)} async-done(((bf16[1,1024,256]{2,1,0:T(8,128)(2,1)}), bf16[1,4096,256]{2,1,0:T(8,128)(2,1)}) %all-gather.4.cloned.1.call-update) | async-done | bytes 2097168 | tf_op jit(solution)/shard_map/all_gather | solution.py:22
  64.7 9.8 %while.14 = (s32[]{:T(128)}, f32[4,128,256]{2,1,0:T(8,128)S(1)}, s32[4,4]{0,1:T(4,128)S(1)}, bf16[4,4,3,128,128]{4,3,2,0,1:T(8,128)(2,1)S(1)}, bf16[4,8,128,256]...) while((s32[]{:T(128)}, f32[4,128,256]{2,1,0:T(8,128)S(1)}, ...), condition=%wide.region_1.2_spmd.clone, body=%wide.region_0.1_spmd.clone.sunk | while | flops 101123120 | bytes 4854827 | solution.py:38
  64.7 1.1 dynamic-slice_bitcast_fusion.2
  65.8 0.1 copy.22
  65.9 0.1 reshape.106
  66.0 0.6 gather_fusion
  66.6 0.1 iota_compare_fusion.2
  66.7 0.4 fusion.23
  67.2 1.1 dynamic-slice_bitcast_fusion.2
  68.3 0.1 copy.22
  68.4 0.1 reshape.106
  68.5 0.6 gather_fusion
  69.1 0.1 iota_compare_fusion.2
  69.2 0.4 fusion.23
  69.6 1.1 dynamic-slice_bitcast_fusion.2
  70.7 0.1 copy.22
  70.8 0.1 reshape.106
  70.9 0.6 gather_fusion
  71.5 0.1 iota_compare_fusion.2
  71.6 0.4 fusion.23
  72.1 1.1 dynamic-slice_bitcast_fusion.2
  73.2 0.1 copy.22
  73.2 0.1 reshape.106
  73.3 0.6 gather_fusion
  74.0 0.1 iota_compare_fusion.2
  74.0 0.4 fusion.23
  74.5 0.0 copy-start.2
  74.5 0.0 copy-start.7
  74.5 0.0 copy-start.8
  74.5 0.1 fusion.9
  74.7 8.6 %all_gather.11 = bf16[1024,256]{1,0:T(8,128)(2,1)S(1)} all-gather(bf16[512,256]{1,0:T(8,128)(2,1)S(1)} %fusion.9), channel_id=1, replica_groups=mesh['row'=4,'replica'=4,'feat'=2] {'feat'}, dimensions={0}, use_global_device_ids=true | all-gather | bytes 786432 | tf_op jit(solution)/shard_map/all_gather | solution.py:40
  83.2 0.0 copy-done
  83.2 0.0 copy-done.2
  83.2 0.4 fusion.13
  83.6 30.5 %all-reduce = (f32[128]{0:T(128)S(1)}, f32[128]{0:T(128)S(1)}) all-reduce(f32[128]{0:T(128)S(1)} %get-tuple-element.166, f32[128]{0:T(128)S(1)} %get-tuple-element.165), channel_id=1, replica_groups=mesh['row'=4,'replica'=4,'feat'=2] {'row','replica'}, use_global_device_ids=true, to_apply=%region_5.6 | all-reduce | flops 256 | bytes 2048 | tf_op jit(solution)/shard_map/psum | solution.py:44
  114.2 0.0 copy-done.7
  114.2 0.0 copy-done.8
  114.2 0.8 fusion.12
  (15 shorter events, 0.1 us)
Async XLA Ops:
  6.5 76.7 %copy-start = (bf16[256,128]{1,0:T(8,128)(2,1)S(1)}, bf16[256,128]{1,0:T(8,128)(2,1)}, u32[]{:S(2)}) copy-start(bf16[256,128]{1,0:T(8,128)(2,1)} %param.17) | copy-start | bytes 196612
  6.5 58.2 %all-gather.4.cloned.1.call-start = ((), (), s32[]{:S(2)}) async-start(), calls=%async_computation | async-start | bytes 2621440 | tf_op jit(solution)/shard_map/all_gather | solution.py:22
  18.6 1.6 %copy-start.4 = (s32[1,4,4,3]{2,1,3,0:T(4,128)S(1)}, s32[1,4,4,3]{2,1,3,0:T(4,128)}, u32[]{:S(2)}) copy-start(s32[1,4,4,3]{2,1,3,0:T(4,128)} %param.13) | copy-start | bytes 580
  18.6 1.7 %copy-start.5 = (s32[1,4,4]{2,1,0:T(4,128)S(1)}, s32[1,4,4]{2,1,0:T(4,128)}, u32[]{:S(2)}) copy-start(s32[1,4,4]{2,1,0:T(4,128)} %param.14) | copy-start | bytes 196
  18.6 1.8 %copy-start.6 = (s32[1,512]{1,0:T(1,128)S(1)}, s32[1,512]{1,0:T(1,128)}, u32[]{:S(2)}) copy-start(s32[1,512]{1,0:T(1,128)} %param.15) | copy-start | bytes 6148
  18.6 1.8 %copy-start.1 = (bf16[1,1024,256]{2,1,0:T(8,128)(2,1)S(1)}, bf16[1,1024,256]{2,1,0:T(8,128)(2,1)}, u32[]{:S(2)}) copy-start(bf16[1,1024,256]{2,1,0:T(8,128)(2,1)} %all-gather) | copy-start | bytes 1572868
  18.7 1.8 %copy-start.3 = (bf16[256,128]{1,0:T(8,128)(2,1)S(1)}, bf16[256,128]{1,0:T(8,128)(2,1)}, u32[]{:S(2)}) copy-start(bf16[256,128]{1,0:T(8,128)(2,1)} %param.16) | copy-start | bytes 196612
  74.5 8.7 %copy-start.2 = (f32[1024,128]{1,0:T(8,128)S(1)}, f32[1024,128]{1,0:T(8,128)}, u32[]{:S(2)}) copy-start(f32[1024,128]{1,0:T(8,128)} %fusion.10) | copy-start | bytes 1572868
  74.5 39.7 %copy-start.7 = (f32[128]{0:T(128)S(1)}, f32[128]{0:T(128)}, u32[]{:S(2)}) copy-start(f32[128]{0:T(128)} %param.19) | copy-start | bytes 1540
  74.5 39.7 %copy-start.8 = (f32[128]{0:T(128)S(1)}, f32[128]{0:T(128)}, u32[]{:S(2)}) copy-start(f32[128]{0:T(128)} %param.18) | copy-start | bytes 1540
Sparse Core Ops, SparseCore 0:
  18.7 45.9 all-gather.3
where the time goes:
time: 122 us
  blocking collectives  51.1 us (42%)
  waiting for transfers between devices  43.2 us (35%)
  between operations  13.5 us (11%)
  local copies, waits for them, and re-layouts  9.28 us (8%)
  matrix products  3.2 us (3%)
  other arithmetic  1.35 us (1%)
    all_gather x1, waiting for transfers between devices, per_device(): piece = lax.all_gather(pair, 'row', axis=0, tiled=True)  43.2 us
    psum x1, blocking collectives, per_device(): lax.psum((jnp.sum(pre, axis=0), jnp.sum(pre * pre, axis=0)), ('row', 'rep...  30.5 us
    all_gather x1, blocking collectives, per_device(): pair = lax.all_gather(local_x, 'feat', axis=0, tiled=True)  12 us
    all_gather x1, blocking collectives, per_device(): agg_pair = lax.all_gather(agg, 'feat', axis=0, tiled=True)  8.55 us
    squeeze x4, local copies, waits for them, and re-layouts, one_shard(): shard = lax.dynamic_index_in_dim(shards, step, 0, keepdims=False)  4.32 us
  transfers between devices with their start and end apart: 1, of which 1 were waited for; matrix products, arithmetic and copies ran while one was open for 2% of the time, Pallas kernels for 0%

commit v1 on v0

--- a/solution.py
+++ b/solution.py
@@ -42,7 +42,7 @@
         agg_pair, w_neigh, preferred_element_type=jnp.float32
     )
     col_sum, col_sq = lax.psum(
-        (jnp.sum(pre, axis=0), jnp.sum(pre * pre, axis=0)), ("row", "replica")
+        lax.psum((jnp.sum(pre, axis=0), jnp.sum(pre * pre, axis=0)), "row"), "replica"
     )
     total_nodes = pre.shape[0] * lax.axis_size("row") * lax.axis_size("replica")
     mean = col_sum / total_nodes

time: 122 us -> 107 us (0.88)
  blocking collectives: 51.1 us -> 36.3 us
    psum x1 -> x2, blocking collectives: 30.5 us -> 15.7 us  [the longest x1 10.1 us: per_device(): lax.psum((jnp.sum(pre, axis=0), jnp.sum(pre * pre, axis=0)), 'row')]
  transfers between devices with their start and end apart: 1 -> 1, of which waited for: 1 -> 1; matrix products, arithmetic and copies ran while one was open for 2% -> 3% of each run, Pallas kernels for 0% -> 0%
where the time goes in v1:
time: 107 us
  waiting for transfers between devices  43.2 us (40%)
  blocking collectives  36.3 us (34%)
  between operations  13.5 us (13%)
  local copies, waits for them, and re-layouts  9.28 us (9%)
  matrix products  3.2 us (3%)
  other arithmetic  1.35 us (1%)
    all_gather x1, waiting for transfers between devices, per_device(): piece = lax.all_gather(pair, 'row', axis=0, tiled=True)  43.2 us
    all_gather x1, blocking collectives, per_device(): pair = lax.all_gather(local_x, 'feat', axis=0, tiled=True)  12 us
    psum x1, blocking collectives, per_device(): lax.psum((jnp.sum(pre, axis=0), jnp.sum(pre * pre, axis=0)), 'row')  10.1 us
    all_gather x1, blocking collectives, per_device(): agg_pair = lax.all_gather(agg, 'feat', axis=0, tiled=True)  8.54 us
    psum x1, blocking collectives, per_device(): lax.psum(lax.psum((jnp.sum(pre, axis=0), jnp.sum(pre * pre, axis=0)), 'ro...  5.65 us
    squeeze x4, local copies, waits for them, and re-layouts, one_shard(): shard = lax.dynamic_index_in_dim(shards, step, 0, keepdims=False)  4.32 us
    gather x4, local copies, waits for them, and re-layouts, one_shard(): picked = shard[cols_now]  2.39 us
  transfers between devices with their start and end apart: 1, of which 1 were waited for; matrix products, arithmetic and copies ran while one was open for 3% of the time, Pallas kernels for 0%

profile of v1, /device:TPU:0, one launch (start us, length us, event | category | flops | bytes accessed | tf_op | source)
XLA Modules:
  0.0 107.0 jit_solution(4621469488110404667)
XLA Ops:
  6.5 0.0 copy-start
  6.5 0.0 all-gather.4.cloned.1.call-start
  6.5 12.0 %all-gather = bf16[1,1024,256]{2,1,0:T(8,128)(2,1)} all-gather(bf16[1,512,256]{2,1,0:T(8,128)(2,1)} %param.11), channel_id=2, replica_groups=mesh['row'=4,'replica'=4,'feat'=2] {'feat'}, dimensions={1}, use_global_device_ids=true | all-gather | bytes 786432 | tf_op jit(solution)/shard_map/all_gather | solution.py:17
  18.6 0.0 all-gather.4.cloned.1.call-update
  18.6 0.0 copy-start.4
  18.6 0.0 copy-start.5
  18.6 0.0 copy-start.6
  18.6 0.0 copy-start.1
  18.6 0.0 copy-start.3
  18.7 1.6 %copy.20 = bf16[1,4,4,3,128,128]{5,4,3,1,2,0:T(8,128)(2,1)S(1)} copy(bf16[1,4,4,3,128,128]{5,4,3,2,1,0:T(8,128)(2,1)} %param.12) | data formatting | bytes 3145728 | tf_op args[1]
  20.2 0.0 copy-done.4
  20.2 0.1 copy.17
  20.4 0.0 copy-done.5
  20.4 0.1 copy.16
  20.4 0.0 copy-done.6
  20.5 0.0 copy-done.1
  20.5 0.0 copy-done.3
  20.5 1.1 %fusion.10 = f32[1024,128]{1,0:T(8,128)} fusion(bf16[256,128]{1,0:T(8,128)(2,1)S(1)} %copy-done.3, bf16[1,1024,256]{2,1,0:T(8,128)(2,1)S(1)} %copy-done.1), kind=kOutput, calls=%fused_computation.20 | convolution fusion | flops 67108864 | bytes 1114112 | tf_op jit(solution)/shard_map/dot_general | solution.py:41
  21.6 43.2 %all-gather.4.cloned.1.call-done = bf16[1,4096,256]{2,1,0:T(8,128)(2,1)} async-done(((bf16[1,1024,256]{2,1,0:T(8,128)(2,1)}), bf16[1,4096,256]{2,1,0:T(8,128)(2,1)}) %all-gather.4.cloned.1.call-update) | async-done | bytes 2097168 | tf_op jit(solution)/shard_map/all_gather | solution.py:22
  64.7 9.8 %while.14 = (s32[]{:T(128)}, f32[4,128,256]{2,1,0:T(8,128)S(1)}, s32[4,4]{0,1:T(4,128)S(1)}, bf16[4,4,3,128,128]{4,3,2,0,1:T(8,128)(2,1)S(1)}, bf16[4,8,128,256]...) while((s32[]{:T(128)}, f32[4,128,256]{2,1,0:T(8,128)S(1)}, ...), condition=%wide.region_1.2_spmd.clone, body=%wide.region_0.1_spmd.clone.sunk | while | flops 101123120 | bytes 4854827 | solution.py:38
  64.7 1.1 %dynamic-slice_bitcast_fusion.2 = bf16[8,128,256]{2,1,0:T(8,128)(2,1)S(1)} fusion(bf16[4,8,128,256]{3,2,1,0:T(8,128)(2,1)} %get-tuple-element.243, s32[]{:T(128)} %get-tuple-element.231), kind=kLoop, calls=%fused_computation.4.clone.1 | loop fusion | bytes 1048580 | tf_op jit(solution)/shard_map/while/body/eval_jaxpr/jit(dynamic_index_in_dim)/squeeze | solution.py:27
  65.8 0.1 copy.22
  65.9 0.1 reshape.106
  66.0 0.6 gather_fusion
  66.6 0.1 iota_compare_fusion.2
  66.7 0.4 fusion.23
  67.2 1.1 %dynamic-slice_bitcast_fusion.2 = bf16[8,128,256]{2,1,0:T(8,128)(2,1)S(1)} fusion(bf16[4,8,128,256]{3,2,1,0:T(8,128)(2,1)} %get-tuple-element.243, s32[]{:T(128)} %get-tuple-element.231), kind=kLoop, calls=%fused_computation.4.clone.1 | loop fusion | bytes 1048580 | tf_op jit(solution)/shard_map/while/body/eval_jaxpr/jit(dynamic_index_in_dim)/squeeze | solution.py:27
  68.3 0.1 copy.22
  68.4 0.1 reshape.106
  68.5 0.6 gather_fusion
  69.1 0.1 iota_compare_fusion.2
  69.2 0.4 fusion.23
  69.6 1.1 %dynamic-slice_bitcast_fusion.2 = bf16[8,128,256]{2,1,0:T(8,128)(2,1)S(1)} fusion(bf16[4,8,128,256]{3,2,1,0:T(8,128)(2,1)} %get-tuple-element.243, s32[]{:T(128)} %get-tuple-element.231), kind=kLoop, calls=%fused_computation.4.clone.1 | loop fusion | bytes 1048580 | tf_op jit(solution)/shard_map/while/body/eval_jaxpr/jit(dynamic_index_in_dim)/squeeze | solution.py:27
  70.7 0.1 copy.22
  70.8 0.1 reshape.106
  70.9 0.6 gather_fusion
  71.5 0.1 iota_compare_fusion.2
  71.6 0.4 fusion.23
  72.1 1.1 %dynamic-slice_bitcast_fusion.2 = bf16[8,128,256]{2,1,0:T(8,128)(2,1)S(1)} fusion(bf16[4,8,128,256]{3,2,1,0:T(8,128)(2,1)} %get-tuple-element.243, s32[]{:T(128)} %get-tuple-element.231), kind=kLoop, calls=%fused_computation.4.clone.1 | loop fusion | bytes 1048580 | tf_op jit(solution)/shard_map/while/body/eval_jaxpr/jit(dynamic_index_in_dim)/squeeze | solution.py:27
  73.2 0.1 copy.22
  73.2 0.1 reshape.106
  73.3 0.6 gather_fusion
  74.0 0.1 iota_compare_fusion.2
  74.0 0.4 fusion.23
  74.5 0.0 copy-start.2
  74.5 0.0 copy-start.7
  74.5 0.0 copy-start.8
  74.5 0.1 fusion.9
  74.7 8.5 %all_gather.11 = bf16[1024,256]{1,0:T(8,128)(2,1)S(1)} all-gather(bf16[512,256]{1,0:T(8,128)(2,1)S(1)} %fusion.9), channel_id=1, replica_groups=mesh['row'=4,'replica'=4,'feat'=2] {'feat'}, dimensions={0}, use_global_device_ids=true | all-gather | bytes 786432 | tf_op jit(solution)/shard_map/all_gather | solution.py:40
  83.2 0.0 copy-done
  83.2 0.0 copy-done.2
  83.2 0.4 fusion.13
  83.6 10.1 %all-reduce.1 = (f32[128]{0:T(128)S(1)}, f32[128]{0:T(128)S(1)}) all-reduce(f32[128]{0:T(128)S(1)} %get-tuple-element.166, f32[128]{0:T(128)S(1)} %get-tuple-element.165), channel_id=1, replica_groups=mesh['row'=4,'replica'=4,'feat'=2] {'row'}, use_global_device_ids=true, to_apply=%region_6.7 | all-reduce | flops 256 | bytes 2048 | tf_op jit(solution)/shard_map/psum | solution.py:45
  93.7 5.6 %all-reduce = (f32[128]{0:T(128)S(1)}, f32[128]{0:T(128)S(1)}) all-reduce(f32[128]{0:T(128)S(1)} %get-tuple-element.181, f32[128]{0:T(128)S(1)} %get-tuple-element.182), channel_id=1, replica_groups=mesh['row'=4,'replica'=4,'feat'=2] {'replica'}, use_global_device_ids=true, to_apply=%region_7.8 | all-reduce | flops 256 | bytes 2048 | tf_op jit(solution)/shard_map/psum | solution.py:44
  99.3 0.0 copy-done.7
  99.3 0.0 copy-done.8
  99.3 0.8 fusion.12
  (15 shorter events, 0.1 us)
Async XLA Ops:
  6.5 76.7 %copy-start = (bf16[256,128]{1,0:T(8,128)(2,1)S(1)}, bf16[256,128]{1,0:T(8,128)(2,1)}, u32[]{:S(2)}) copy-start(bf16[256,128]{1,0:T(8,128)(2,1)} %param.17) | copy-start | bytes 196612
  6.5 58.2 %all-gather.4.cloned.1.call-start = ((), (), s32[]{:S(2)}) async-start(), calls=%async_computation | async-start | bytes 2621440 | tf_op jit(solution)/shard_map/all_gather | solution.py:22
  18.6 1.6 %copy-start.4 = (s32[1,4,4,3]{2,1,3,0:T(4,128)S(1)}, s32[1,4,4,3]{2,1,3,0:T(4,128)}, u32[]{:S(2)}) copy-start(s32[1,4,4,3]{2,1,3,0:T(4,128)} %param.13) | copy-start | bytes 580
  18.6 1.7 %copy-start.5 = (s32[1,4,4]{2,1,0:T(4,128)S(1)}, s32[1,4,4]{2,1,0:T(4,128)}, u32[]{:S(2)}) copy-start(s32[1,4,4]{2,1,0:T(4,128)} %param.14) | copy-start | bytes 196
  18.6 1.8 %copy-start.6 = (s32[1,512]{1,0:T(1,128)S(1)}, s32[1,512]{1,0:T(1,128)}, u32[]{:S(2)}) copy-start(s32[1,512]{1,0:T(1,128)} %param.15) | copy-start | bytes 6148
  18.6 1.8 %copy-start.1 = (bf16[1,1024,256]{2,1,0:T(8,128)(2,1)S(1)}, bf16[1,1024,256]{2,1,0:T(8,128)(2,1)}, u32[]{:S(2)}) copy-start(bf16[1,1024,256]{2,1,0:T(8,128)(2,1)} %all-gather) | copy-start | bytes 1572868
  18.6 1.8 %copy-start.3 = (bf16[256,128]{1,0:T(8,128)(2,1)S(1)}, bf16[256,128]{1,0:T(8,128)(2,1)}, u32[]{:S(2)}) copy-start(bf16[256,128]{1,0:T(8,128)(2,1)} %param.16) | copy-start | bytes 196612
  74.5 8.7 %copy-start.2 = (f32[1024,128]{1,0:T(8,128)S(1)}, f32[1024,128]{1,0:T(8,128)}, u32[]{:S(2)}) copy-start(f32[1024,128]{1,0:T(8,128)} %fusion.10) | copy-start | bytes 1572868
  74.5 24.8 %copy-start.7 = (f32[128]{0:T(128)S(1)}, f32[128]{0:T(128)}, u32[]{:S(2)}) copy-start(f32[128]{0:T(128)} %param.19) | copy-start | bytes 1540
  74.5 24.8 %copy-start.8 = (f32[128]{0:T(128)S(1)}, f32[128]{0:T(128)}, u32[]{:S(2)}) copy-start(f32[128]{0:T(128)} %param.18) | copy-start | bytes 1540
Sparse Core Ops, SparseCore 0:
  18.7 45.9 all-gather.3
